TPU v7x, 32 devices: a whole 2x2x4 slice. The times are simulated.
32 devices in a mesh: section: 8 (over z, core), ctx: 4 (over y, x).
Axes of the slice: x: 2, y: 2, z: 4, core: 2. Of those that a mesh axis runs over, the one named last changes fastest.
Arguments:
- gate_q: bfloat16 [8, 512, 4096], P('section', 'ctx'), may hold values from -6 to 6
- gate_k: bfloat16 [8, 512, 4096], P('section', 'ctx'), may hold values from -6 to 6
- value_in: bfloat16 [8, 512, 4096], P('section', 'ctx'), may hold values from -6 to 6
- filter_raw: bfloat16 [8, 512, 4096], P('section', 'ctx'), may hold values from -0.5 to 0.5
- decay_rate: float32 [8, 4096], P('section'), may hold values from 0.25 to 16
- skip_gain: float32 [8, 4096], P('section'), may hold values from -4 to 4
- grad_out: bfloat16 [8, 512, 4096], P('section', 'ctx'), may hold values from -6 to 6
Outputs:
- grad_q: bfloat16 [8, 512, 4096], P('section', 'ctx')
- grad_k: bfloat16 [8, 512, 4096], P('section', 'ctx')
- grad_passed: bfloat16 [8, 512, 4096], P('section', 'ctx')
- filter_grad: bfloat16 [8, 512, 4096], P('section', 'ctx')
- rate_grad: float32 [8, 4096], P('section')
- skip_grad: float32 [8, 4096], P('section')
All inputs are finite; a program needn't handle non-finite values.
Results may differ from a plain program's by a relative error of at most 0.013.
Values may be sent and summed in bfloat16 or wider, within the bound.
A program may use at most 128 MiB of HBM per device.

v0:
```python
import math

import jax
import jax.numpy as jnp
from jax import lax
from jax.sharding import PartitionSpec as P

exact_mode = lax.Precision.HIGHEST


def shifted(x, axis, by):
    size = lax.axis_size(axis)
    pairs = [(i, i + by) for i in range(size) if 0 <= i + by < size]
    return lax.ppermute(x, axis, pairs)


def every_table(parts_count):
    twice = 2 * parts_count
    m_index = jnp.arange(parts_count, dtype=jnp.int32)[:, None, None]
    bin_grid = jnp.arange(twice, dtype=jnp.int32).reshape(parts_count, 2).T[None]
    angle = (m_index * bin_grid % twice).astype(jnp.float32) * (math.pi / parts_count)
    return jnp.stack([jnp.cos(angle), -jnp.sin(angle)], axis=2)


def combined_tables(slot_bins, tok_rows, fft_length):
    factor_len = fft_length // tok_rows
    row_index = jnp.arange(tok_rows, dtype=jnp.int32)
    frequency = slot_bins[:, None] + factor_len * row_index[None, :]
    product = row_index[None, :, None] * frequency[:, None, :] % fft_length
    angle = product.astype(jnp.float32) * (2.0 * math.pi / fft_length)
    cosine = jnp.cos(angle)
    sine = jnp.sin(angle)
    forward_table = jnp.stack(
        [jnp.stack([cosine, -sine], axis=2), jnp.stack([sine, cosine], axis=2)], axis=1
    )
    cos_back = jnp.transpose(cosine, (0, 2, 1))
    sin_back = jnp.transpose(sine, (0, 2, 1))
    inverse_table = jnp.stack(
        [jnp.stack([cos_back, sin_back], axis=2), jnp.stack([-sin_back, cos_back], axis=2)], axis=1
    )
    return (forward_table, inverse_table)


def spectral_middle(stack_mixed, stack_filter, stack_pulled, slot_bins, tok_rows, fft_length):
    forward_table, inverse_table = combined_tables(slot_bins, tok_rows, fft_length)

    def forward(stacked):
        return jnp.einsum(
            "spjc,spjqb->sqbc", stacked.astype(jnp.float32), forward_table, precision=exact_mode
        )

    def inverse(real_part, imag_part):
        stacked = jnp.stack([real_part, imag_part], axis=1)
        return jnp.einsum("sqbc,sqbpj->spjc", stacked, inverse_table, precision=exact_mode).astype(
            jnp.bfloat16
        )

    spec_mix = forward(stack_mixed)
    spec_fil = forward(stack_filter)
    spec_pul = forward(stack_pulled)
    mix_real, mix_imag = (spec_mix[:, 0], spec_mix[:, 1])
    fil_real, fil_imag = (spec_fil[:, 0], spec_fil[:, 1])
    pul_real, pul_imag = (spec_pul[:, 0], spec_pul[:, 1])
    folded_conv = inverse(
        fil_real * mix_real - fil_imag * mix_imag, fil_real * mix_imag + fil_imag * mix_real
    )
    folded_adj = inverse(
        fil_real * pul_real + fil_imag * pul_imag, fil_real * pul_imag - fil_imag * pul_real
    )
    folded_cor = inverse(
        mix_real * pul_real + mix_imag * pul_imag, mix_real * pul_imag - mix_imag * pul_real
    )
    return (folded_conv, folded_adj, folded_cor)


def shards(gate_q, gate_k, value_in, filter_raw, decay_rate, skip_gain, grad_out):
    parts_count = lax.axis_size("ctx")
    my_rank = lax.axis_index("ctx")
    tok_rows = gate_q.shape[1]
    channels = gate_q.shape[2]
    group_rows = tok_rows // parts_count
    seq_length = tok_rows * parts_count
    fft_length = 2 * seq_length
    positions = (my_rank * tok_rows + jnp.arange(tok_rows, dtype=jnp.int32)).astype(
        jnp.float32
    ) / seq_length
    rate_row = decay_rate[0][None, :]
    skip_row = skip_gain[0][None, :]
    envelope = jnp.exp(-rate_row * positions[:, None])
    modulated = filter_raw[0].astype(jnp.float32) * envelope
    filter_bf = modulated.astype(jnp.bfloat16)
    mixed_in = (gate_k[0].astype(jnp.float32) * value_in[0].astype(jnp.float32)).astype(
        jnp.bfloat16
    )
    pulled = (gate_q[0].astype(jnp.float32) * grad_out[0].astype(jnp.float32)).astype(jnp.bfloat16)
    block_shape = (parts_count, group_rows, channels)
    sectioned_mixed, sectioned_filter, sectioned_pulled = (
        lax.all_to_all(
            mixed_in.reshape(block_shape), "ctx", split_axis=0, concat_axis=0, tiled=True
        ),
        lax.all_to_all(
            filter_bf.reshape(block_shape), "ctx", split_axis=0, concat_axis=0, tiled=True
        ),
        lax.all_to_all(pulled.reshape(block_shape), "ctx", split_axis=0, concat_axis=0, tiled=True),
    )
    table_first = every_table(parts_count)

    def first_section(sectioned):
        return jnp.einsum(
            "mgc,mlir->lirgc", sectioned.astype(jnp.float32), table_first, precision=exact_mode
        ).astype(jnp.bfloat16)

    got_mixed, got_filter, got_pulled = (
        lax.all_to_all(
            first_section(sectioned_mixed), "ctx", split_axis=2, concat_axis=2, tiled=True
        ),
        lax.all_to_all(
            first_section(sectioned_filter), "ctx", split_axis=2, concat_axis=2, tiled=True
        ),
        lax.all_to_all(
            first_section(sectioned_pulled), "ctx", split_axis=2, concat_axis=2, tiled=True
        ),
    )

    def unpack(received):
        return received.reshape(2, 2, tok_rows, channels)

    slot_bins = 2 * my_rank + jnp.arange(2, dtype=jnp.int32)
    folded_conv, folded_adj, folded_cor = spectral_middle(
        unpack(got_mixed), unpack(got_filter), unpack(got_pulled), slot_bins, tok_rows, fft_length
    )

    def pack(folded):
        return folded.reshape(2, 2, parts_count, group_rows, channels)

    back_conv, back_adj, back_cor = (
        lax.all_to_all(pack(folded_conv), "ctx", split_axis=2, concat_axis=2, tiled=True),
        lax.all_to_all(pack(folded_adj), "ctx", split_axis=2, concat_axis=2, tiled=True),
        lax.all_to_all(pack(folded_cor), "ctx", split_axis=2, concat_axis=2, tiled=True),
    )
    table_last = table_first / fft_length

    def last_section(received):
        return jnp.einsum(
            "lirgc,mlir->mgc", received.astype(jnp.float32), table_last, precision=exact_mode
        ).astype(jnp.bfloat16)

    home_conv, home_adj, home_cor = (
        lax.all_to_all(last_section(back_conv), "ctx", split_axis=0, concat_axis=0, tiled=True),
        lax.all_to_all(last_section(back_adj), "ctx", split_axis=0, concat_axis=0, tiled=True),
        lax.all_to_all(last_section(back_cor), "ctx", split_axis=0, concat_axis=0, tiled=True),
    )
    conv_out = home_conv.reshape(tok_rows, channels).astype(jnp.float32)
    adjoint = home_adj.reshape(tok_rows, channels).astype(jnp.float32)
    filter_corr = home_cor.reshape(tok_rows, channels).astype(jnp.float32)
    mixed_f = mixed_in.astype(jnp.float32)
    pulled_f = pulled.astype(jnp.float32)
    grad_q_local = (grad_out[0].astype(jnp.float32) * (conv_out + skip_row * mixed_f)).astype(
        jnp.bfloat16
    )
    mixed_grad = adjoint + skip_row * pulled_f
    grad_k_local = (mixed_grad * value_in[0].astype(jnp.float32)).astype(jnp.bfloat16)
    passing = (mixed_grad * gate_k[0].astype(jnp.float32)).astype(jnp.bfloat16)
    passed = shifted(passing[None], "section", -1)
    filter_local = (filter_corr * envelope).astype(jnp.bfloat16)
    rate_part = -jnp.sum(positions[:, None] * filter_corr * modulated, axis=0)
    skip_part = jnp.sum(mixed_f * pulled_f, axis=0)
    rate_total, skip_total = (
        lax.psum(rate_part.astype(jnp.bfloat16), "ctx").astype(jnp.float32),
        lax.psum(skip_part.astype(jnp.bfloat16), "ctx").astype(jnp.float32),
    )
    return (
        grad_q_local[None],
        grad_k_local[None],
        passed,
        filter_local[None],
        rate_total[None],
        skip_total[None],
    )


def solution(mesh):
    in_specs = (
        P("section", "ctx", None),
        P("section", "ctx", None),
        P("section", "ctx", None),
        P("section", "ctx", None),
        P("section", None),
        P("section", None),
        P("section", "ctx", None),
    )
    out_specs = (
        P("section", "ctx", None),
        P("section", "ctx", None),
        P("section", "ctx", None),
        P("section", "ctx", None),
        P("section", None),
        P("section", None),
    )
    return jax.shard_map(shards, mesh=mesh, in_specs=in_specs, out_specs=out_specs, check_vma=False)
```

profile of v0, /device:TPU:0, one launch (start us, length us, event | category | flops | bytes accessed | tf_op | source)
XLA Modules:
  0.0 480.6 jit_solution(238260348380390639)
XLA Ops:
  4.2 5.2 %all-to-all-start = ((bf16[4,32,4096]{2,1,0:T(8,128)(2,1)}), bf16[4,32,4096]{2,1,0:T(8,128)(2,1)S(1)}, u32[]{:S(2)}, u32[]{:S(2)}) async-start(bf16[4,32,4096]{2,1,0:T(8,128)(2,1)} %fusion.21), calls=%async_computation | async-start | bytes 2097152 | tf_op jit(solution)/shard_map/all_to_all | solution.py:101
  13.0 10.0 %all-to-all-done = bf16[4,32,4096]{2,1,0:T(8,128)(2,1)S(1)} async-done(((bf16[4,32,4096]{2,1,0:T(8,128)(2,1)}), bf16[4,32,4096]{2,1,0:T(8,128)(2,1)S(1)}, u32[]{:S(2)}, u32[]{:S(2)}) %all-to-all-start) | async-done | bytes 1048608 | tf_op jit(solution)/shard_map/all_to_all | solution.py:101
  26.5 13.1 %all-to-all-done.6 = bf16[4,32,4096]{2,1,0:T(8,128)(2,1)S(1)} async-done(((bf16[4,32,4096]{2,1,0:T(8,128)(2,1)}), bf16[4,32,4096]{2,1,0:T(8,128)(2,1)S(1)}, u32[]{:S(2)}, u32[]{:S(2)}) %all-to-all-start.6) | async-done | bytes 1048608 | tf_op jit(solution)/shard_map/all_to_all | solution.py:104
  43.2 6.4 %convolution_convert_fusion = bf16[2,2,4,32,4096]{4,2,3,1,0:T(4,128)(2,1)S(1)} fusion(bf16[4,32,4096,1,1]{2,1,0,4,3:T(8,128)(2,1)S(1)} %bitcast.132, f32[4,2,1,4]{0,3,2,1:T(4,128)S(1)} %get-tuple-element.33, f32[4,2,1,4]{0,3,2,1:T(4,128)S(1)} %get-tuple-element.32), kind=kOutput, calls=%fused_computation.15 | convolution fusion | flops 102760512 | bytes 5243136 | tf_op jit(solution)/shard_map/mgc,mlir->lirgc/dot_general | solution.py:109
  61.3 6.4 %convolution_convert_fusion.2 = bf16[2,2,4,32,4096]{4,2,3,1,0:T(4,128)(2,1)S(1)} fusion(bf16[4,32,4096,1,1]{2,1,0,4,3:T(8,128)(2,1)S(1)} %bitcast.128, f32[4,2,1,4]{0,3,2,1:T(4,128)S(1)} %get-tuple-element.33, f32[4,2,1,4]{0,3,2,1:T(4,128)S(1)} %get-tuple-element.32), kind=kOutput, calls=%fused_computation.17 | convolution fusion | flops 102760512 | bytes 5243136 | tf_op jit(solution)/shard_map/mgc,mlir->lirgc/dot_general | solution.py:109
  72.0 36.1 %all-to-all-done.7 = bf16[2,2,4,32,4096]{4,3,1,0,2:T(8,128)(2,1)} async-done(((bf16[2,2,4,32,4096]{4,3,1,0,2:T(8,128)(2,1)}), bf16[2,2,4,32,4096]{4,3,1,0,2:T(8,128)(2,1)}, u32[]{:S(2)}, u32[]{:S(2)}) %all-to-all-start.7) | async-done | bytes 4194336 | tf_op jit(solution)/shard_map/all_to_all | solution.py:120
  108.1 5.4 %all-to-all-start.1 = ((bf16[2,2,4,32,4096]{4,3,1,0,2:T(8,128)(2,1)}), bf16[2,2,4,32,4096]{4,3,1,0,2:T(8,128)(2,1)}, u32[]{:S(2)}, u32[]{:S(2)}) async-start(bf16[2,2,4,32,4096]{4,3,1,0,2:T(8,128)(2,1)} %copy.44), calls=%async_computation.1 | async-start | bytes 8388608 | tf_op jit(solution)/shard_map/all_to_all | solution.py:117
  113.6 6.4 %convolution_convert_fusion.1 = bf16[2,2,4,32,4096]{4,2,3,1,0:T(4,128)(2,1)S(1)} fusion(bf16[4,32,4096,1,1]{2,1,0,4,3:T(8,128)(2,1)S(1)} %bitcast.130, f32[4,2,1,4]{0,3,2,1:T(4,128)S(1)} %get-tuple-element.33, f32[4,2,1,4]{0,3,2,1:T(4,128)S(1)} %get-tuple-element.32), kind=kOutput, calls=%fused_computation.16 | convolution fusion | flops 102760512 | bytes 5243136 | tf_op jit(solution)/shard_map/mgc,mlir->lirgc/dot_general | solution.py:109
  124.2 36.2 %all-to-all-done.1 = bf16[2,2,4,32,4096]{4,3,1,0,2:T(8,128)(2,1)} async-done(((bf16[2,2,4,32,4096]{4,3,1,0,2:T(8,128)(2,1)}), bf16[2,2,4,32,4096]{4,3,1,0,2:T(8,128)(2,1)}, u32[]{:S(2)}, u32[]{:S(2)}) %all-to-all-start.1) | async-done | bytes 4194336 | tf_op jit(solution)/shard_map/all_to_all | solution.py:117
  171.7 5.6 %convolution_bitcast_fusion.2 = f32[2,2,128,4096]{3,2,1,0:T(8,128)} fusion(bf16[2,2,128,4096,1]{3,2,1,4,0:T(8,128)(2,1)S(1)} %bitcast.121, f32[2,1,128,2,128]{2,4,1,3,0:T(8,128)S(1)} %get-tuple-element.24, f32[2,1,128,2,128]{2,4,1,3,0:T(8,128)S(1)} %get-tuple-element.23), kind=kOutput, calls=%fused_computation.14 | convolution fusion | flops 6442582016 | bytes 13107200 | tf_op jit(solution)/shard_map/spjc,spjqb->sqbc/dot_general | solution.py:48
  177.3 5.7 %convolution_bitcast_fusion = f32[2,2,128,4096]{3,2,1,0:T(8,128)} fusion(bf16[2,2,128,4096,1]{3,2,1,4,0:T(8,128)(2,1)S(1)} %bitcast.119, f32[2,1,128,2,128]{2,4,1,3,0:T(8,128)S(1)} %get-tuple-element.24, f32[2,1,128,2,128]{2,4,1,3,0:T(8,128)S(1)} %get-tuple-element.23), kind=kOutput, calls=%fused_computation.12 | convolution fusion | flops 6442582016 | bytes 13107200 | tf_op jit(solution)/shard_map/spjc,spjqb->sqbc/dot_general | solution.py:48
  183.0 29.4 %all-to-all-done.3 = bf16[2,2,4,32,4096]{4,3,1,0,2:T(8,128)(2,1)} async-done(((bf16[2,2,4,32,4096]{4,3,1,0,2:T(8,128)(2,1)}), bf16[2,2,4,32,4096]{4,3,1,0,2:T(8,128)(2,1)}, u32[]{:S(2)}, u32[]{:S(2)}) %all-to-all-start.3) | async-done | bytes 4194336 | tf_op jit(solution)/shard_map/all_to_all | solution.py:114
  215.0 5.7 %convolution_bitcast_fusion.1 = f32[2,2,128,4096]{3,2,1,0:T(8,128)} fusion(bf16[2,2,128,4096,1]{3,2,1,4,0:T(8,128)(2,1)S(1)} %bitcast.120, f32[2,1,128,2,128]{2,4,1,3,0:T(8,128)S(1)} %get-tuple-element.24, f32[2,1,128,2,128]{2,4,1,3,0:T(8,128)S(1)} %get-tuple-element.23), kind=kOutput, calls=%fused_computation.13 | convolution fusion | flops 6442582016 | bytes 13107200 | tf_op jit(solution)/shard_map/spjc,spjqb->sqbc/dot_general | solution.py:48
  220.7 11.1 %multiply_add_fusion = (f32[2,1,128,4096]{3,2,1,0:T(8,128)S(1)}, f32[2,1,128,4096]{3,2,1,0:T(8,128)}, f32[2,1,128,4096]{3,2,1,0:T(8,128)}, f32[2,1,128,4096]{3,2,1,0:T(8,128)}) fusion(f32[2,2,128,4096]{3,2,1,0:T(8,128)} %convolution_bitcast_fusion, f32[2,2,128,4096]{3,2,1,0:T(8,128)} %convolution_bitcast_fusion.1, f32[2,2,128,4096]{3,2,1,0:T(8,128)S(1)} %bitcast.118), kind=kLoop, calls=%fused_computation.25 | loop fusion | flops 12582912 | bytes 41943040 | tf_op jit(solution)/shard_map/add | solution.py:71
  231.9 7.5 %maximum_bitcast_fusion = (f32[2,2,128,4096,1]{3,2,1,0,4:T(8,128)S(1)}, f32[2,2,128,4096,1]{3,2,1,0,4:T(8,128)}) fusion(f32[2,1,128,4096]{3,2,1,0:T(8,128)} %get-tuple-element.17, f32[2,1,128,4096]{3,2,1,0:T(8,128)} %get-tuple-element.18, f32[2,1,128,4096]{3,2,1,0:T(8,128)} %get-tuple-element.12, f32[2,1,128,4096]{3,2,1,0:T(8,128)S(1)} %get-tuple-element.11), kind=kLoop, calls=%fused_computation | loop fusion | flops 4194304 | bytes 33554432 | tf_op jit(solution)/shard_map/stack | solution.py:53
  239.4 8.0 %fusion.4 = bf16[2,2,128,4096,1]{3,2,1,0,4:T(8,128)(2,1)S(1)} fusion(f32[2,2,128,4096,1]{3,2,1,0,4:T(8,128)S(1)} %get-tuple-element.34, f32[2,1,128,2,128]{2,4,3,0,1:T(8,128)S(1)} %get-tuple-element.22, f32[2,1,128,2,128]{2,4,3,0,1:T(8,128)S(1)} %get-tuple-element.21), kind=kOutput, calls=%fused_computation.10 | convolution fusion | flops 6442582016 | bytes 13107200 | tf_op jit(solution)/shard_map/sqbc,sqbpj->spjc/dot_general | solution.py:54
  247.9 6.3 %copy.51 = bf16[2,2,4,32,4096]{4,0,1,3,2:T(2,128)(2,1)} copy(bf16[2,2,4,32,4096]{4,3,2,0,1:T(8,128)(2,1)S(1)} %bitcast.122) | data formatting | bytes 8388608 | tf_op jit(solution)/shard_map/reshape | solution.py:134
  259.4 9.2 %fusion = bf16[2,2,128,4096,1]{3,2,1,0,4:T(8,128)(2,1)S(1)} fusion(f32[2,2,128,4096,1]{3,2,1,0,4:T(8,128)} %get-tuple-element.35, f32[2,1,128,2,128]{2,4,3,0,1:T(8,128)S(1)} %get-tuple-element.22, f32[2,1,128,2,128]{2,4,3,0,1:T(8,128)S(1)} %get-tuple-element.21), kind=kOutput, calls=%fused_computation.4 | convolution fusion | flops 6442582016 | bytes 13107200 | tf_op jit(solution)/shard_map/sqbc,sqbpj->spjc/dot_general | solution.py:54
  269.1 6.4 %copy.66 = bf16[2,2,4,32,4096]{4,0,1,3,2:T(2,128)(2,1)} copy(bf16[2,2,4,32,4096]{4,3,2,0,1:T(8,128)(2,1)S(1)} %bitcast.123) | data formatting | bytes 8388608 | tf_op jit(solution)/shard_map/reshape | solution.py:134
  275.5 30.8 %all-to-all-done.4 = bf16[2,2,4,32,4096]{4,0,1,3,2:T(2,128)(2,1)} async-done(((bf16[2,2,4,32,4096]{4,0,1,3,2:T(2,128)(2,1)}), bf16[2,2,4,32,4096]{4,0,1,3,2:T(2,128)(2,1)}, u32[]{:S(2)}, u32[]{:S(2)}) %all-to-all-start.4) | async-done | bytes 4194336 | tf_op jit(solution)/shard_map/all_to_all | solution.py:137
  306.3 5.3 %all-to-all-start.10 = ((bf16[2,2,4,32,4096]{4,0,1,3,2:T(2,128)(2,1)}), bf16[2,2,4,32,4096]{4,0,1,3,2:T(2,128)(2,1)}, u32[]{:S(2)}, u32[]{:S(2)}) async-start(bf16[2,2,4,32,4096]{4,0,1,3,2:T(2,128)(2,1)} %copy.66), calls=%async_computation.10 | async-start | bytes 8388608 | tf_op jit(solution)/shard_map/all_to_all | solution.py:139
  311.6 6.5 %multiply_add_fusion.1 = (f32[2,1,128,4096]{3,2,1,0:T(8,128)S(1)}, f32[2,1,128,4096]{3,2,1,0:T(8,128)S(1)}) fusion(f32[2,2,128,4096]{3,2,1,0:T(8,128)} %convolution_bitcast_fusion, f32[2,2,128,4096]{3,2,1,0:T(8,128)} %convolution_bitcast_fusion.2), kind=kLoop, calls=%fused_computation.27 | loop fusion | flops 6291456 | bytes 25165824 | tf_op jit(solution)/shard_map/add | solution.py:68
  318.1 7.8 %fusion.2 = bf16[2,2,128,4096,1]{3,2,1,0,4:T(8,128)(2,1)S(1)} fusion(f32[2,1,128,2,128]{2,4,3,0,1:T(8,128)S(1)} %get-tuple-element.22, f32[2,1,128,2,128]{2,4,3,0,1:T(8,128)S(1)} %get-tuple-element.21, f32[2,1,128,4096]{3,2,1,0:T(8,128)S(1)} %get-tuple-element.14, f32[2,1,128,4096]{3,2,1,0:T(8,128)S(1)} %get-tuple-element.13), kind=kOutput, calls=%fused_computation.7 | convolution fusion | flops 6444679168 | bytes 13107200 | tf_op jit(solution)/shard_map/sqbc,sqbpj->spjc/dot_general | solution.py:54
  326.5 6.3 %copy.60 = bf16[2,2,4,32,4096]{4,0,1,3,2:T(2,128)(2,1)} copy(bf16[2,2,4,32,4096]{4,3,2,0,1:T(8,128)(2,1)S(1)} %bitcast.124) | data formatting | bytes 8388608 | tf_op jit(solution)/shard_map/reshape | solution.py:134
  332.8 25.7 %all-to-all-done.10 = bf16[2,2,4,32,4096]{4,0,1,3,2:T(2,128)(2,1)} async-done(((bf16[2,2,4,32,4096]{4,0,1,3,2:T(2,128)(2,1)}), bf16[2,2,4,32,4096]{4,0,1,3,2:T(2,128)(2,1)}, u32[]{:S(2)}, u32[]{:S(2)}) %all-to-all-start.10) | async-done | bytes 4194336 | tf_op jit(solution)/shard_map/all_to_all | solution.py:139
  363.6 10.8 %fusion.6 = bf16[4,32,4096]{2,0,1:T(4,128)(2,1)S(1)} fusion(bf16[2,2,4,32,4096]{4,0,1,3,2:T(2,128)(2,1)} %all-to-all-done.4, f32[4,2,1,4]{0,3,2,1:T(4,128)S(1)} %get-tuple-element.33, f32[4,2,1,4]{0,3,2,1:T(4,128)S(1)} %get-tuple-element.32), kind=kOutput, calls=%fused_computation.21 | convolution fusion | flops 101187712 | bytes 5243136 | tf_op jit(solution)/shard_map/lirgc,mlir->mgc/dot_general | solution.py:144
  375.9 34.5 %all-to-all-done.8 = bf16[2,2,4,32,4096]{4,0,1,3,2:T(2,128)(2,1)} async-done(((bf16[2,2,4,32,4096]{4,0,1,3,2:T(2,128)(2,1)}), bf16[2,2,4,32,4096]{4,0,1,3,2:T(2,128)(2,1)}, u32[]{:S(2)}, u32[]{:S(2)}) %all-to-all-start.8) | async-done | bytes 4194336 | tf_op jit(solution)/shard_map/all_to_all | solution.py:138
  414.0 10.8 %fusion.7 = bf16[4,32,4096]{2,0,1:T(4,128)(2,1)S(1)} fusion(bf16[2,2,4,32,4096]{4,0,1,3,2:T(2,128)(2,1)} %all-to-all-done.8, f32[4,2,1,4]{0,3,2,1:T(4,128)S(1)} %get-tuple-element.33, f32[4,2,1,4]{0,3,2,1:T(4,128)S(1)} %get-tuple-element.32), kind=kOutput, calls=%fused_computation.22 | convolution fusion | flops 101187712 | bytes 5243136 | tf_op jit(solution)/shard_map/lirgc,mlir->mgc/dot_general | solution.py:144
  430.8 10.8 %fusion.8 = bf16[4,32,4096]{2,0,1:T(4,128)(2,1)S(1)} fusion(bf16[2,2,4,32,4096]{4,0,1,3,2:T(2,128)(2,1)} %all-to-all-done.10, f32[4,2,1,4]{0,3,2,1:T(4,128)S(1)} %get-tuple-element.33, f32[4,2,1,4]{0,3,2,1:T(4,128)S(1)} %get-tuple-element.32), kind=kOutput, calls=%fused_computation.23 | convolution fusion | flops 101187712 | bytes 5243136 | tf_op jit(solution)/shard_map/lirgc,mlir->mgc/dot_general | solution.py:144
  447.4 5.5 %fusion.14 = (bf16[1,128,4096]{2,1,0:T(8,128)(2,1)}, bf16[1,128,4096]{2,1,0:T(8,128)(2,1)}, bf16[1,128,4096]{2,1,0:T(8,128)(2,1)}) fusion(bf16[1,128,4096]{2,1,0:T(8,128)(2,1)} %param.8, bf16[1,128,4096]{2,1,0:T(8,128)(2,1)} %get-tuple-element.9, f32[4096]{0:T(1024)S(1)} %bitcast.136, bf16[1,128,4096]{2,1,0:T(8,128)(2,1)} %param.9, ...), kind=kLoop, calls=%fused_computation.43 | loop fusion | flops 8912896 | bytes 10502144 | tf_op jit(solution)/shard_map/convert_element_type | solution.py:163
  454.2 6.2 %all-to-all-done.11 = bf16[4,32,4096]{2,1,0:T(8,128)(2,1)S(1)} async-done(((bf16[4,32,4096]{2,1,0:T(8,128)(2,1)}), bf16[4,32,4096]{2,1,0:T(8,128)(2,1)S(1)}, u32[]{:S(2)}, u32[]{:S(2)}) %all-to-all-start.11) | async-done | bytes 1048608 | tf_op jit(solution)/shard_map/all_to_all | solution.py:151
  461.2 15.3 %all-reduce = (bf16[1,4096]{1,0:T(2,128)(2,1)S(1)}, bf16[1,4096]{1,0:T(2,128)(2,1)S(1)}) all-reduce(bf16[1,4096]{1,0:T(2,128)(2,1)S(1)} %broadcast_in_dim.10, bf16[1,4096]{1,0:T(2,128)(2,1)S(1)} %broadcast_in_dim.12), channel_id=1, replica_groups=mesh['section'=8,'ctx'=4] {'ctx'}, use_global_device_ids=true, to_apply=%region_1.2 | all-reduce | flops 8192 | bytes 32768 | tf_op jit(solution)/shard_map/psum | solution.py:169
  (63 shorter events, 82.8 us)
Async XLA Ops:
  0.6 8.7 %copy-start.3 = (bf16[1,128,4096]{2,1,0:T(8,128)(2,1)S(1)}, bf16[1,128,4096]{2,1,0:T(8,128)(2,1)}, u32[]{:S(2)}) copy-start(bf16[1,128,4096]{2,1,0:T(8,128)(2,1)} %param.13) | copy-start | bytes 3145732
  0.6 8.7 %copy-start.2 = (bf16[1,128,4096]{2,1,0:T(8,128)(2,1)S(1)}, bf16[1,128,4096]{2,1,0:T(8,128)(2,1)}, u32[]{:S(2)}) copy-start(bf16[1,128,4096]{2,1,0:T(8,128)(2,1)} %param.8) | copy-start | bytes 3145732
  4.2 18.8 %all-to-all-start = ((bf16[4,32,4096]{2,1,0:T(8,128)(2,1)}), bf16[4,32,4096]{2,1,0:T(8,128)(2,1)S(1)}, u32[]{:S(2)}, u32[]{:S(2)}) async-start(bf16[4,32,4096]{2,1,0:T(8,128)(2,1)} %fusion.21), calls=%async_computation | async-start | bytes 2097152 | tf_op jit(solution)/shard_map/all_to_all | solution.py:101
  23.0 16.6 %all-to-all-start.6 = ((bf16[4,32,4096]{2,1,0:T(8,128)(2,1)}), bf16[4,32,4096]{2,1,0:T(8,128)(2,1)S(1)}, u32[]{:S(2)}, u32[]{:S(2)}) async-start(bf16[4,32,4096]{2,1,0:T(8,128)(2,1)} %bitcast.32), calls=%async_computation.6 | async-start | bytes 2097152 | tf_op jit(solution)/shard_map/all_to_all | solution.py:104
  39.6 16.6 %all-to-all-start.2 = ((bf16[4,32,4096]{2,1,0:T(8,128)(2,1)}), bf16[4,32,4096]{2,1,0:T(8,128)(2,1)S(1)}, u32[]{:S(2)}, u32[]{:S(2)}) async-start(bf16[4,32,4096]{2,1,0:T(8,128)(2,1)} %bitcast.17), calls=%async_computation.2 | async-start | bytes 2097152 | tf_op jit(solution)/shard_map/all_to_all | solution.py:98
  56.2 52.0 %all-to-all-start.7 = ((bf16[2,2,4,32,4096]{4,3,1,0,2:T(8,128)(2,1)}), bf16[2,2,4,32,4096]{4,3,1,0,2:T(8,128)(2,1)}, u32[]{:S(2)}, u32[]{:S(2)}) async-start(bf16[2,2,4,32,4096]{4,3,1,0,2:T(8,128)(2,1)} %copy.56), calls=%async_computation.7 | async-start | bytes 8388608 | tf_op jit(solution)/shard_map/all_to_all | solution.py:120
  108.1 52.3 %all-to-all-start.1 = ((bf16[2,2,4,32,4096]{4,3,1,0,2:T(8,128)(2,1)}), bf16[2,2,4,32,4096]{4,3,1,0,2:T(8,128)(2,1)}, u32[]{:S(2)}, u32[]{:S(2)}) async-start(bf16[2,2,4,32,4096]{4,3,1,0,2:T(8,128)(2,1)} %copy.44), calls=%async_computation.1 | async-start | bytes 8388608 | tf_op jit(solution)/shard_map/all_to_all | solution.py:117
  160.5 52.0 %all-to-all-start.3 = ((bf16[2,2,4,32,4096]{4,3,1,0,2:T(8,128)(2,1)}), bf16[2,2,4,32,4096]{4,3,1,0,2:T(8,128)(2,1)}, u32[]{:S(2)}, u32[]{:S(2)}) async-start(bf16[2,2,4,32,4096]{4,3,1,0,2:T(8,128)(2,1)} %copy.47), calls=%async_computation.3 | async-start | bytes 8388608 | tf_op jit(solution)/shard_map/all_to_all | solution.py:114
  212.4 8.3 %slice-start = ((s8[8388608]{0:T(1024)(128)(4,1)}), s8[4194304]{0:T(1024)(128)(4,1)S(1)}, s32[]{:S(2)}) async-start(s8[8388608]{0:T(1024)(128)(4,1)} %bitcast.117), calls=%async_computation.12 | async-start | bytes 8388608
  215.0 5.7 %slice-start.1 = ((s8[8388608]{0:T(1024)(128)(4,1)}), s8[4194304]{0:T(1024)(128)(4,1)S(1)}, s32[]{:S(2)}) async-start(s8[8388608]{0:T(1024)(128)(4,1)} %bitcast.117), calls=%async_computation.13 | async-start | bytes 8388608
  254.2 52.0 %all-to-all-start.4 = ((bf16[2,2,4,32,4096]{4,0,1,3,2:T(2,128)(2,1)}), bf16[2,2,4,32,4096]{4,0,1,3,2:T(2,128)(2,1)}, u32[]{:S(2)}, u32[]{:S(2)}) async-start(bf16[2,2,4,32,4096]{4,0,1,3,2:T(2,128)(2,1)} %copy.51), calls=%async_computation.4 | async-start | bytes 8388608 | tf_op jit(solution)/shard_map/all_to_all | solution.py:137
  306.3 52.2 %all-to-all-start.10 = ((bf16[2,2,4,32,4096]{4,0,1,3,2:T(2,128)(2,1)}), bf16[2,2,4,32,4096]{4,0,1,3,2:T(2,128)(2,1)}, u32[]{:S(2)}, u32[]{:S(2)}) async-start(bf16[2,2,4,32,4096]{4,0,1,3,2:T(2,128)(2,1)} %copy.66), calls=%async_computation.10 | async-start | bytes 8388608 | tf_op jit(solution)/shard_map/all_to_all | solution.py:139
  358.5 52.0 %all-to-all-start.8 = ((bf16[2,2,4,32,4096]{4,0,1,3,2:T(2,128)(2,1)}), bf16[2,2,4,32,4096]{4,0,1,3,2:T(2,128)(2,1)}, u32[]{:S(2)}, u32[]{:S(2)}) async-start(bf16[2,2,4,32,4096]{4,0,1,3,2:T(2,128)(2,1)} %copy.60), calls=%async_computation.8 | async-start | bytes 8388608 | tf_op jit(solution)/shard_map/all_to_all | solution.py:138
  410.4 16.6 %all-to-all-start.5 = ((bf16[4,32,4096]{2,1,0:T(8,128)(2,1)}), bf16[4,32,4096]{2,1,0:T(8,128)(2,1)S(1)}, u32[]{:S(2)}, u32[]{:S(2)}) async-start(bf16[4,32,4096]{2,1,0:T(8,128)(2,1)} %copy.54), calls=%async_computation.5 | async-start | bytes 2097152 | tf_op jit(solution)/shard_map/all_to_all | solution.py:149
  427.1 16.8 %all-to-all-start.9 = ((bf16[4,32,4096]{2,1,0:T(8,128)(2,1)}), bf16[4,32,4096]{2,1,0:T(8,128)(2,1)S(1)}, u32[]{:S(2)}, u32[]{:S(2)}) async-start(bf16[4,32,4096]{2,1,0:T(8,128)(2,1)} %copy.63), calls=%async_computation.9 | async-start | bytes 2097152 | tf_op jit(solution)/shard_map/all_to_all | solution.py:150
  441.7 5.8 %copy-start.4 = (f32[1,4096]{1,0:T(1,128)S(1)}, f32[1,4096]{1,0:T(1,128)}, u32[]{:S(2)}) copy-start(f32[1,4096]{1,0:T(1,128)} %param.12) | copy-start | bytes 49156
  443.8 3.6 copy-start.1
  443.8 16.6 %all-to-all-start.11 = ((bf16[4,32,4096]{2,1,0:T(8,128)(2,1)}), bf16[4,32,4096]{2,1,0:T(8,128)(2,1)S(1)}, u32[]{:S(2)}, u32[]{:S(2)}) async-start(bf16[4,32,4096]{2,1,0:T(8,128)(2,1)} %copy.69), calls=%async_computation.11 | async-start | bytes 2097152 | tf_op jit(solution)/shard_map/all_to_all | solution.py:151
  447.4 13.0 %copy-start = (bf16[1,128,4096]{2,1,0:T(8,128)(2,1)S(1)}, bf16[1,128,4096]{2,1,0:T(8,128)(2,1)}, u32[]{:S(2)}) copy-start(bf16[1,128,4096]{2,1,0:T(8,128)(2,1)} %param.10) | copy-start | bytes 3145732
  452.9 26.4 %collective-permute-start = (bf16[1,128,4096]{2,1,0:T(8,128)(2,1)}, bf16[1,128,4096]{2,1,0:T(8,128)(2,1)S(1)}, u32[]{:S(2)}, u32[]{:S(2)}) collective-permute-start(bf16[1,128,4096]{2,1,0:T(8,128)(2,1)} %get-tuple-element.19), channel_id=1, source_target_pairs={{4,0},{8,4},{12,8},{16,12},{20,16},{24,20},{28,24},{5,1},{9,5},{13... | collective-permute-start | bytes 3145736 | tf_op jit(solution)/shard_map/ppermute | solution.py:14
where the time goes:
time: 489 us; the launch traced here: 481 us
  waiting for transfers between devices  226 us (46%)
  matrix products  93.5 us (19%)
  starting transfers between devices  55.5 us (11%)
  local copies, waits for them, and re-layouts  46.6 us (10%)
  other arithmetic  42.8 us (9%)
  blocking collectives  15.3 us (3%)
    all_to_all x1, waiting for transfers between devices, shards(): lax.all_to_all(first_section(sectioned_filter), 'ctx', split_axis=2, conc...  36.2 us
    all_to_all x1, waiting for transfers between devices, shards(): lax.all_to_all(first_section(sectioned_pulled), 'ctx', split_axis=2, conc...  36.1 us
    all_to_all x1, waiting for transfers between devices, shards(): lax.all_to_all(pack(folded_adj), 'ctx', split_axis=2, concat_axis=2, tile...  34.5 us
    dot_general x3, matrix products, last_section(): jnp.einsum('lirgc,mlir->mgc', received.astype(jnp.float32), table_last, p...  32.4 us
    all_to_all x1, waiting for transfers between devices, shards(): lax.all_to_all(pack(folded_conv), 'ctx', split_axis=2, concat_axis=2, til...  30.8 us
    all_to_all x1, waiting for transfers between devices, shards(): lax.all_to_all(first_section(sectioned_mixed), 'ctx', split_axis=2, conca...  29.4 us
    all_to_all x1, waiting for transfers between devices, shards(): lax.all_to_all(pack(folded_cor), 'ctx', split_axis=2, concat_axis=2, tile...  25.7 us
    dot_general x3, matrix products, inverse(): jnp.einsum('sqbc,sqbpj->spjc', stacked, inverse_table, precision=exact_mode)  25 us
  transfers between devices with their start and end apart: 13, of which 12 were waited for; matrix products, arithmetic and copies ran while one was open for 28% of the time, Pallas kernels for 0%

commit v1 on v0

v1 whole, which is shorter than its diff:
```python
import functools
import math

import jax
import jax.numpy as jnp
import numpy as np
from jax import lax
from jax.experimental import pallas as pl
from jax.experimental.pallas import tpu as pltpu
from jax.sharding import PartitionSpec as P

MESH = pl.DeviceIdType.MESH
F32 = jnp.float32
BF16 = jnp.bfloat16


def make_tables(n, rows):
    length = 2 * n * rows
    half = rows // 2
    j = np.arange(rows)[None, :]
    b = np.arange(rows)[:, None]

    def angle(a):
        return 2.0 * np.pi * ((j * (a + 2 * n * b)) % length) / length

    fwd = np.zeros((n, 2 * rows, 2 * rows))
    inv = np.zeros((n, 2 * rows, 2 * rows))
    for a in range(1, n):
        c, s = np.cos(angle(a)), np.sin(angle(a))
        fwd[a] = np.block([[c, s], [-s, c]])
        inv[a] = np.block([[c.T, -s.T], [s.T, c.T]]) * (2.0 / length)
    for slot, a in ((0, 0), (1, n)):
        c, s = np.cos(angle(a))[:half], np.sin(angle(a))[:half]
        weight = np.full((half, 1), 2.0 / length)
        re_rows = slice(slot * half, (slot + 1) * half)
        im_rows = slice(rows + slot * half, rows + (slot + 1) * half)
        cols = slice(slot * rows, (slot + 1) * rows)
        im = -s
        if slot == 0:
            im = im.copy()
            im[0] = np.cos(np.pi * np.arange(rows))
            weight[0] = 1.0 / length
        fwd[0, re_rows, cols] = c
        fwd[0, im_rows, cols] = im
        inv[0, cols, re_rows] = (c * weight).T
        inv[0, cols, im_rows] = (im * weight).T
    return fwd, inv


def scaled(coef, x):
    if abs(coef - 1.0) < 1e-12:
        return x
    if abs(coef + 1.0) < 1e-12:
        return -x
    return x * np.float32(coef)


def combine(terms, zero):
    total = None
    for coef, x in terms:
        if abs(coef) < 1e-12:
            continue
        if total is None:
            total = scaled(coef, x)
        elif coef < 0:
            total = total - scaled(-coef, x)
        else:
            total = total + scaled(coef, x)
    return zero if total is None else total


def kernel(
    n, nsec, chunk, steps,
    gq_ref, gk_ref, vi_ref, fr_ref, go_ref, rate_ref, skip_ref, fwd_ref, inv_ref,
    oq_ref, ok_ref, op_ref, of_ref, orate_ref, oskip_ref,
    sbuf, rbuf, obuf, hbuf, pbuf, part, fold, sstat, gstat,
    s_send, s_recv, o_send, o_recv, p_send, p_recv, t_send, t_recv,
):
    rows = gq_ref.shape[0]
    width = chunk * steps
    seq = rows * n
    me = lax.axis_index("ctx")
    sec = lax.axis_index("section")
    before = lax.rem(sec + nsec - 1, nsec)
    after = lax.rem(sec + 1, nsec)

    barrier = pltpu.get_barrier_semaphore()
    for o in range(1, n):
        pl.semaphore_signal(
            barrier, inc=1, device_id={"ctx": lax.rem(me + o, n)}, device_id_type=MESH
        )
    for other in (before, after):
        pl.semaphore_signal(barrier, inc=1, device_id={"section": other}, device_id_type=MESH)
    pl.semaphore_wait(barrier, n + 1)

    def columns(owner, k):
        return pl.ds(pl.multiple_of(owner * width + k * chunk, chunk), chunk)

    def here(row0, count):
        row = lax.broadcasted_iota(jnp.int32, (count, 1), 0) + (row0 + me * rows)
        return row.astype(F32) * np.float32(1.0 / seq)

    def send_in(k, d):
        return pltpu.make_async_remote_copy(
            src_ref=sbuf.at[k, d], dst_ref=rbuf.at[k, me], send_sem=s_send.at[k, d],
            recv_sem=s_recv.at[k, me], device_id={"ctx": d}, device_id_type=MESH,
        )

    def got_in(k, m):
        return pltpu.make_async_remote_copy(
            src_ref=sbuf.at[k, m], dst_ref=rbuf.at[k, m], send_sem=s_send.at[k, m],
            recv_sem=s_recv.at[k, m], device_id={"ctx": m}, device_id_type=MESH,
        )

    def send_out(k, m):
        return pltpu.make_async_remote_copy(
            src_ref=obuf.at[k, m], dst_ref=hbuf.at[k, me], send_sem=o_send.at[k, m],
            recv_sem=o_recv.at[k, me], device_id={"ctx": m}, device_id_type=MESH,
        )

    def got_out(k, m):
        return pltpu.make_async_remote_copy(
            src_ref=obuf.at[k, m], dst_ref=hbuf.at[k, m], send_sem=o_send.at[k, m],
            recv_sem=o_recv.at[k, m], device_id={"ctx": m}, device_id_type=MESH,
        )

    def send_stat(d):
        return pltpu.make_async_remote_copy(
            src_ref=sstat, dst_ref=gstat.at[me], send_sem=t_send.at[d],
            recv_sem=t_recv.at[me], device_id={"ctx": d}, device_id_type=MESH,
        )

    def got_stat(m):
        return pltpu.make_async_remote_copy(
            src_ref=sstat, dst_ref=gstat.at[m], send_sem=t_send.at[m],
            recv_sem=t_recv.at[m], device_id={"ctx": m}, device_id_type=MESH,
        )

    def pass_copy(k, m):
        return pltpu.make_async_remote_copy(
            src_ref=pbuf.at[k, m], dst_ref=op_ref.at[:, columns(m, k)], send_sem=p_send.at[k, m],
            recv_sem=p_recv.at[k, m], device_id={"section": before}, device_id_type=MESH,
        )

    @pl.loop(0, steps * n)
    def _(i):
        k, o = i // n, lax.rem(i, n)
        d = lax.rem(me + 1 + o, n)
        cols = columns(d, k)
        mixed = (gk_ref[:, cols].astype(F32) * vi_ref[:, cols].astype(F32)).astype(BF16)
        pulled = (gq_ref[:, cols].astype(F32) * go_ref[:, cols].astype(F32)).astype(BF16)
        envelope = jnp.exp(-rate_ref[:, cols] * here(0, rows))
        filt = (fr_ref[:, cols].astype(F32) * envelope).astype(BF16)
        sbuf[k, d, :, 0:chunk] = mixed
        sbuf[k, d, :, chunk:2 * chunk] = filt
        sbuf[k, d, :, 2 * chunk:3 * chunk] = pulled

        @pl.when(o < n - 1)
        def _():
            send_in(k, d).start()

        @pl.when(o == n - 1)
        def _():
            rbuf[k, me, :, 0:chunk] = mixed
            rbuf[k, me, :, chunk:2 * chunk] = filt
            rbuf[k, me, :, 2 * chunk:3 * chunk] = pulled

    @pl.when(sec == nsec - 1)
    def _():
        op_ref[...] = jnp.zeros_like(op_ref)

    tile = 16
    top = lax.broadcasted_iota(jnp.int32, (rows, 1), 0)

    @pl.loop(0, steps)
    def _(k):
        @pl.loop(0, n - 1)
        def _(o):
            got_in(k, lax.rem(me + 1 + o, n)).wait_recv()

        @pl.loop(0, rows // tile)
        def _(t):
            at = pl.ds(pl.multiple_of(t * tile, tile), tile)
            low = pl.ds(pl.multiple_of(rows + t * tile, tile), tile)
            for g in range(3):
                lanes = slice(g * chunk, (g + 1) * chunk)
                x = [rbuf[k, m, at, lanes].astype(F32) for m in range(n)]
                zero = jnp.zeros_like(x[0])
                even = combine([(1.0, x[m]) for m in range(0, n, 2)], zero)
                odd = combine([(1.0, x[m]) for m in range(1, n, 2)], zero)
                part[0, at, lanes] = (even + odd).astype(BF16)
                part[0, low, lanes] = (even - odd).astype(BF16)
                for a in range(1, n // 2 + 1):
                    cos = [math.cos(math.pi * m * a / n) for m in range(n)]
                    sin = [math.sin(math.pi * m * a / n) for m in range(n)]
                    ce = combine([(cos[m], x[m]) for m in range(0, n, 2)], zero)
                    co = combine([(cos[m], x[m]) for m in range(1, n, 2)], zero)
                    se = combine([(sin[m], x[m]) for m in range(0, n, 2)], zero)
                    so = combine([(sin[m], x[m]) for m in range(1, n, 2)], zero)
                    part[a, at, lanes] = (ce + co).astype(BF16)
                    part[a, low, lanes] = (-se - so).astype(BF16)
                    if n - a != a:
                        part[n - a, at, lanes] = (ce - co).astype(BF16)
                        part[n - a, low, lanes] = (se - so).astype(BF16)

        @pl.loop(0, n)
        def _(a):
            spec = jnp.dot(fwd_ref[a], part[a], preferred_element_type=F32)
            mr, fr, pr = (spec[:rows, g * chunk:(g + 1) * chunk] for g in range(3))
            mi, fi, pi = (spec[rows:, g * chunk:(g + 1) * chunk] for g in range(3))
            real_pair = jnp.logical_and(top == 0, a == 0)

            def product(ar, ai, br, bi, sign):
                cross = ai * bi
                re = ar * br + jnp.where(real_pair, 0.0, sign * cross)
                im = jnp.where(real_pair, cross, ar * bi - sign * ai * br)
                return re, im

            outs = (
                product(fr, fi, mr, mi, -1.0),
                product(fr, fi, pr, pi, 1.0),
                product(mr, mi, pr, pi, 1.0),
            )
            for g in range(3):
                lanes = slice(g * chunk, (g + 1) * chunk)
                part[a, 0:rows, lanes] = outs[g][0].astype(BF16)
                part[a, rows:2 * rows, lanes] = outs[g][1].astype(BF16)
            fold[a] = jnp.dot(inv_ref[a], part[a], preferred_element_type=F32)

        def unfold(t, carry):
            rate_sum, skip_sum = carry
            at = pl.ds(pl.multiple_of(t * tile, tile), tile)
            low = pl.ds(pl.multiple_of(rows + t * tile, tile), tile)
            for g in range(3):
                lanes = slice(g * chunk, (g + 1) * chunk)
                re = [fold[a, at, lanes] for a in range(n)]
                im = [fold[a, low, lanes] for a in range(n)]
                zero = jnp.zeros_like(re[0])
                for m in range(n):
                    terms = [(1.0, re[0]), ((-1.0) ** m, im[0])]
                    for a in range(1, n):
                        terms.append((math.cos(math.pi * m * a / n), re[a]))
                        terms.append((-math.sin(math.pi * m * a / n), im[a]))
                    value = combine(terms, zero).astype(BF16)
                    obuf[k, m, at, lanes] = value
                    if g == 2:
                        when = lax.broadcasted_iota(jnp.int32, (tile, 1), 0) + (t * tile + m * rows)
                        when = when.astype(F32) * np.float32(1.0 / seq)
                        mixed = rbuf[k, m, at, 0:chunk].astype(F32)
                        filt = rbuf[k, m, at, chunk:2 * chunk].astype(F32)
                        pulled = rbuf[k, m, at, 2 * chunk:3 * chunk].astype(F32)
                        rate_sum = rate_sum + when * value.astype(F32) * filt
                        skip_sum = skip_sum + mixed * pulled
            return rate_sum, skip_sum

        start = jnp.zeros((tile, chunk), F32)
        rate_sum, skip_sum = lax.fori_loop(0, rows // tile, unfold, (start, start))
        mine = pl.ds(pl.multiple_of(k * chunk, chunk), chunk)
        sstat[0:1, mine] = -jnp.sum(rate_sum, axis=0, keepdims=True)
        sstat[1:2, mine] = jnp.sum(skip_sum, axis=0, keepdims=True)

        @pl.loop(0, n - 1)
        def _(o):
            send_out(k, lax.rem(me + 1 + o, n)).start()

        hbuf[k, me] = obuf[k, me]

    for o in range(1, n):
        send_stat(lax.rem(me + o, n)).start()
    gstat[me] = sstat[...]

    @pl.loop(0, steps * n)
    def _(i):
        k, o = i // n, lax.rem(i, n)
        m = lax.rem(me + o, n)

        @pl.when(o > 0)
        def _():
            got_out(k, m).wait_recv()

        cols = columns(m, k)
        conv = hbuf[k, m, :, 0:chunk].astype(F32)
        adjoint = hbuf[k, m, :, chunk:2 * chunk].astype(F32)
        corr = hbuf[k, m, :, 2 * chunk:3 * chunk].astype(F32)
        mixed = sbuf[k, m, :, 0:chunk].astype(F32)
        pulled = sbuf[k, m, :, 2 * chunk:3 * chunk].astype(F32)
        skip = skip_ref[:, cols]
        oq_ref[:, cols] = (go_ref[:, cols].astype(F32) * (conv + skip * mixed)).astype(BF16)
        mixed_grad = adjoint + skip * pulled
        pbuf[k, m] = (mixed_grad * gk_ref[:, cols].astype(F32)).astype(BF16)

        @pl.when(sec > 0)
        def _():
            pass_copy(k, m).start()

        ok_ref[:, cols] = (mixed_grad * vi_ref[:, cols].astype(F32)).astype(BF16)
        envelope = jnp.exp(-rate_ref[:, cols] * here(0, rows))
        of_ref[:, cols] = (corr * envelope).astype(BF16)

    for o in range(1, n):
        got_stat(lax.rem(me + o, n)).wait_recv()
    for m in range(n):
        orate_ref[:, m * width:(m + 1) * width] = gstat[m, 0:1, :]
        oskip_ref[:, m * width:(m + 1) * width] = gstat[m, 1:2, :]

    for o in range(1, n):
        send_stat(lax.rem(me + o, n)).wait_send()

    @pl.loop(0, steps * (n - 1))
    def _(i):
        k, o = i // (n - 1), lax.rem(i, n - 1)
        d = lax.rem(me + 1 + o, n)
        send_in(k, d).wait_send()
        send_out(k, d).wait_send()

    @pl.loop(0, steps * n)
    def _(i):
        k, m = i // n, lax.rem(i, n)

        @pl.when(sec > 0)
        def _():
            pass_copy(k, m).wait_send()

        @pl.when(sec < nsec - 1)
        def _():
            pass_copy(k, m).wait_recv()


def shards(n, nsec, gate_q, gate_k, value_in, filter_raw, decay_rate, skip_gain, grad_out):
    rows, channels = gate_q.shape[1:]
    width = channels // n
    chunk = 128
    steps = width // chunk
    fwd, inv = make_tables(n, rows)
    fwd, inv = jnp.asarray(fwd, BF16), jnp.asarray(inv, BF16)
    block = jax.ShapeDtypeStruct((rows, channels), BF16)
    row = jax.ShapeDtypeStruct((1, channels), F32)
    vmem = pl.BlockSpec(memory_space=pltpu.VMEM)
    message = (steps, n, rows, 3 * chunk)
    dma = pltpu.SemaphoreType.DMA
    outs = pl.pallas_call(
        functools.partial(kernel, n, nsec, chunk, steps),
        out_shape=(block, block, block, block, row, row),
        in_specs=[vmem] * 9,
        out_specs=(vmem,) * 6,
        scratch_shapes=[
            pltpu.VMEM(message, BF16),
            pltpu.VMEM(message, BF16),
            pltpu.VMEM(message, BF16),
            pltpu.VMEM(message, BF16),
            pltpu.VMEM((steps, n, rows, chunk), BF16),
            pltpu.VMEM((n, 2 * rows, 3 * chunk), BF16),
            pltpu.VMEM((n, 2 * rows, 3 * chunk), F32),
            pltpu.VMEM((2, width), F32),
            pltpu.VMEM((n, 2, width), F32),
            dma((steps, n)), dma((steps, n)), dma((steps, n)), dma((steps, n)),
            dma((steps, n)), dma((steps, n)), dma((n,)), dma((n,)),
        ],
        compiler_params=pltpu.CompilerParams(
            collective_id=0, has_side_effects=True, vmem_limit_bytes=50 * 1024 * 1024
        ),
        name="hyena_backward",
    )(
        gate_q[0], gate_k[0], value_in[0], filter_raw[0], grad_out[0],
        decay_rate, skip_gain, fwd, inv,
    )
    oq, ok, op, of, orate, oskip = outs
    return oq[None], ok[None], op[None], of[None], orate, oskip


def solution(mesh):
    n, nsec = mesh.shape["ctx"], mesh.shape["section"]
    tokens = P("section", "ctx", None)
    return jax.shard_map(
        functools.partial(shards, n, nsec),
        mesh=mesh,
        in_specs=(tokens, tokens, tokens, tokens, P("section", None), P("section", None), tokens),
        out_specs=(tokens, tokens, tokens, tokens, P("section", None), P("section", None)),
        check_vma=False,
    )
```

time: 489 us -> 94 us (0.19)
  the two profiles are of different devices: /device:TPU:0 before, /device:TPU:1 now
where the time goes in v1:
time: 94 us; the launch traced here: 93.6 us
  Pallas kernels  83 us (88%)
  local copies, waits for them, and re-layouts  9.87 us (10%)
    pallas_call x1, Pallas kernels, shards(): pl.pallas_call(functools.partial(kernel, n, nsec, chunk, steps), out_shap...  83 us
    unnamed x18, local copies, waits for them, and re-layouts  9.87 us

profile of v1, /device:TPU:1, one launch (start us, length us, event | category | flops | bytes accessed | tf_op | source)
XLA Modules:
  0.0 93.6 jit_solution(17104093586768739483)
XLA Ops:
  0.6 0.0 copy-start
  0.6 1.0 %copy-done = bf16[4,256,256]{2,1,0:T(8,128)(2,1)S(1)} copy-done((bf16[4,256,256]{2,1,0:T(8,128)(2,1)S(1)}, bf16[4,256,256]{2,1,0:T(8,128)(2,1)}, u32[]{:S(2)}) %copy-start) | copy-done | bytes 524312
  1.7 0.0 copy-start.1
  1.7 1.0 %copy-done.1 = bf16[4,256,256]{2,1,0:T(8,128)(2,1)S(1)} copy-done((bf16[4,256,256]{2,1,0:T(8,128)(2,1)S(1)}, bf16[4,256,256]{2,1,0:T(8,128)(2,1)}, u32[]{:S(2)}) %copy-start.1) | copy-done | bytes 524312
  2.7 0.0 copy-start.2
  2.7 0.7 copy-done.2
  3.4 0.0 copy-start.3
  3.4 0.7 copy-done.3
  4.2 83.0 %hyena_backward.1 = (bf16[128,4096]{1,0:T(8,128)(2,1)S(1)}, bf16[128,4096]{1,0:T(8,128)(2,1)S(1)}, bf16[128,4096]{1,0:T(8,128)(2,1)}, bf16[128,4096]{1,0:T(8,128...) custom-call(bf16[128,4096]{1,0:T(8,128)(2,1)} %bitcast.13, bf16[128,4096]{1,0:T(8,128)(2,1)} %bitcast.14, ...), custom_call_target="tpu_custom_call" | custom-call | tf_op jit(solution)/shard_map/hyena_backward/pallas_call | solution.py:341
  87.2 1.0 %copy.21 = bf16[1,128,4096]{2,1,0:T(8,128)(2,1)} copy(bf16[1,128,4096]{2,1,0:T(8,128)(2,1)S(1)} %bitcast.10) | data formatting | bytes 2097152
  88.2 0.0 copy-start.5
  88.2 1.0 %copy.22 = bf16[1,128,4096]{2,1,0:T(8,128)(2,1)} copy(bf16[1,128,4096]{2,1,0:T(8,128)(2,1)S(1)} %bitcast.9) | data formatting | bytes 2097152
  89.1 0.6 copy-done.5
  89.8 0.0 copy-start.4
  89.8 1.0 %copy.23 = bf16[1,128,4096]{2,1,0:T(8,128)(2,1)} copy(bf16[1,128,4096]{2,1,0:T(8,128)(2,1)S(1)} %bitcast.12) | data formatting | bytes 2097152
  90.7 0.6 copy-done.4
  91.4 1.0 %copy.24 = bf16[1,128,4096]{2,1,0:T(8,128)(2,1)} copy(bf16[1,128,4096]{2,1,0:T(8,128)(2,1)S(1)} %bitcast.11) | data formatting | bytes 2097152
  92.4 0.6 copy.25
  93.0 0.6 copy.26
Async XLA Ops:
  0.6 1.0 %copy-start = (bf16[4,256,256]{2,1,0:T(8,128)(2,1)S(1)}, bf16[4,256,256]{2,1,0:T(8,128)(2,1)}, u32[]{:S(2)}) copy-start(bf16[4,256,256]{2,1,0:T(8,128)(2,1)} %constant.5.clone.inv_ref) | copy-start | bytes 1572868
  1.7 1.0 %copy-start.1 = (bf16[4,256,256]{2,1,0:T(8,128)(2,1)S(1)}, bf16[4,256,256]{2,1,0:T(8,128)(2,1)}, u32[]{:S(2)}) copy-start(bf16[4,256,256]{2,1,0:T(8,128)(2,1)} %constant.4.clone.fwd_ref) | copy-start | bytes 1572868
  2.7 0.7 copy-start.2
  3.4 0.7 copy-start.3
  88.2 1.6 %copy-start.5 = (bf16[128,4096]{1,0:T(8,128)(2,1)S(1)}, bf16[128,4096]{1,0:T(8,128)(2,1)}, u32[]{:S(2)}) copy-start(bf16[128,4096]{1,0:T(8,128)(2,1)} %get-tuple-element.14) | copy-start | bytes 3145732
  89.8 1.6 %copy-start.4 = (bf16[128,4096]{1,0:T(8,128)(2,1)S(1)}, bf16[128,4096]{1,0:T(8,128)(2,1)}, u32[]{:S(2)}) copy-start(bf16[128,4096]{1,0:T(8,128)(2,1)} %get-tuple-element.15) | copy-start | bytes 3145732

commit v2 on v1

--- a/solution.py
+++ b/solution.py
@@ -71,8 +71,10 @@
 
 def kernel(
     n, nsec, chunk, steps,
+    gq_hbm, gk_hbm, vi_hbm, fr_hbm, go_hbm, rate_hbm, skip_hbm, fwd_hbm, inv_hbm,
+    oq_hbm, ok_hbm, op_ref, of_hbm, orate_hbm, oskip_hbm,
     gq_ref, gk_ref, vi_ref, fr_ref, go_ref, rate_ref, skip_ref, fwd_ref, inv_ref,
-    oq_ref, ok_ref, op_ref, of_ref, orate_ref, oskip_ref,
+    ostage, zeros, orate_ref, oskip_ref, in_sem, row_sem, out_sem, end_sem,
     sbuf, rbuf, obuf, hbuf, pbuf, part, fold, sstat, gstat,
     s_send, s_recv, o_send, o_recv, p_send, p_recv, t_send, t_recv,
 ):
@@ -84,6 +86,41 @@
     before = lax.rem(sec + nsec - 1, nsec)
     after = lax.rem(sec + 1, nsec)
 
+    def columns(owner, k):
+        return pl.ds(pl.multiple_of(owner * width + k * chunk, chunk), chunk)
+
+    tokens = (
+        (gk_hbm, gk_ref), (vi_hbm, vi_ref), (gq_hbm, gq_ref), (go_hbm, go_ref), (fr_hbm, fr_ref)
+    )
+    whole = (
+        (rate_hbm, rate_ref), (skip_hbm, skip_ref), (fwd_hbm, fwd_ref), (inv_hbm, inv_ref)
+    )
+
+    def load_first(g, d):
+        hbm, ref = tokens[g]
+        return pltpu.make_async_copy(
+            hbm.at[:, columns(d, 0)], ref.at[:, columns(d, 0)], in_sem.at[g, 0, d]
+        )
+
+    def load_rest(g, d):
+        hbm, ref = tokens[g]
+        cols = pl.ds(pl.multiple_of(d * width + chunk, chunk), width - chunk)
+        return pltpu.make_async_copy(hbm.at[:, cols], ref.at[:, cols], in_sem.at[g, 1, d])
+
+    def load_whole(g):
+        return pltpu.make_async_copy(whole[g][0], whole[g][1], row_sem.at[g])
+
+    load_whole(0).start()
+    for o in range(n):
+        for g in range(5):
+            load_first(g, lax.rem(me + 1 + o, n)).start()
+    if steps > 1:
+        for d in range(n):
+            for g in range(5):
+                load_rest(g, d).start()
+    for g in range(1, 4):
+        load_whole(g).start()
+
     barrier = pltpu.get_barrier_semaphore()
     for o in range(1, n):
         pl.semaphore_signal(
@@ -92,9 +129,7 @@
     for other in (before, after):
         pl.semaphore_signal(barrier, inc=1, device_id={"section": other}, device_id_type=MESH)
     pl.semaphore_wait(barrier, n + 1)
-
-    def columns(owner, k):
-        return pl.ds(pl.multiple_of(owner * width + k * chunk, chunk), chunk)
+    load_whole(0).wait()
 
     def here(row0, count):
         row = lax.broadcasted_iota(jnp.int32, (count, 1), 0) + (row0 + me * rows)
@@ -147,6 +182,18 @@
         k, o = i // n, lax.rem(i, n)
         d = lax.rem(me + 1 + o, n)
         cols = columns(d, k)
+
+        @pl.when(k == 0)
+        def _():
+            for g in range(5):
+                load_first(g, d).wait()
+
+        if steps > 1:
+            @pl.when(k == 1)
+            def _():
+                for g in range(5):
+                    load_rest(g, d).wait()
+
         mixed = (gk_ref[:, cols].astype(F32) * vi_ref[:, cols].astype(F32)).astype(BF16)
         pulled = (gq_ref[:, cols].astype(F32) * go_ref[:, cols].astype(F32)).astype(BF16)
         envelope = jnp.exp(-rate_ref[:, cols] * here(0, rows))
@@ -165,9 +212,22 @@
             rbuf[k, me, :, chunk:2 * chunk] = filt
             rbuf[k, me, :, 2 * chunk:3 * chunk] = pulled
 
+    def clear():
+        return pltpu.make_async_copy(zeros, op_ref, end_sem.at[0])
+
     @pl.when(sec == nsec - 1)
     def _():
-        op_ref[...] = jnp.zeros_like(op_ref)
+        zeros[...] = jnp.zeros_like(zeros)
+        clear().start()
+
+    for g in range(1, 4):
+        load_whole(g).wait()
+
+    def store(g, k, m):
+        out = (oq_hbm, ok_hbm, of_hbm)[g]
+        return pltpu.make_async_copy(
+            ostage.at[g, k, m], out.at[:, columns(m, k)], out_sem.at[g, k, m]
+        )
 
     tile = 16
     top = lax.broadcasted_iota(jnp.int32, (rows, 1), 0)
@@ -285,7 +345,7 @@
         mixed = sbuf[k, m, :, 0:chunk].astype(F32)
         pulled = sbuf[k, m, :, 2 * chunk:3 * chunk].astype(F32)
         skip = skip_ref[:, cols]
-        oq_ref[:, cols] = (go_ref[:, cols].astype(F32) * (conv + skip * mixed)).astype(BF16)
+        ostage[0, k, m] = (go_ref[:, cols].astype(F32) * (conv + skip * mixed)).astype(BF16)
         mixed_grad = adjoint + skip * pulled
         pbuf[k, m] = (mixed_grad * gk_ref[:, cols].astype(F32)).astype(BF16)
 
@@ -293,15 +353,24 @@
         def _():
             pass_copy(k, m).start()
 
-        ok_ref[:, cols] = (mixed_grad * vi_ref[:, cols].astype(F32)).astype(BF16)
+        store(0, k, m).start()
+        ostage[1, k, m] = (mixed_grad * vi_ref[:, cols].astype(F32)).astype(BF16)
+        store(1, k, m).start()
         envelope = jnp.exp(-rate_ref[:, cols] * here(0, rows))
-        of_ref[:, cols] = (corr * envelope).astype(BF16)
+        ostage[2, k, m] = (corr * envelope).astype(BF16)
+        store(2, k, m).start()
 
     for o in range(1, n):
         got_stat(lax.rem(me + o, n)).wait_recv()
     for m in range(n):
         orate_ref[:, m * width:(m + 1) * width] = gstat[m, 0:1, :]
         oskip_ref[:, m * width:(m + 1) * width] = gstat[m, 1:2, :]
+    rows_out = (
+        pltpu.make_async_copy(orate_ref, orate_hbm, end_sem.at[1]),
+        pltpu.make_async_copy(oskip_ref, oskip_hbm, end_sem.at[2]),
+    )
+    for copy in rows_out:
+        copy.start()
 
     for o in range(1, n):
         send_stat(lax.rem(me + o, n)).wait_send()
@@ -324,6 +393,33 @@
         @pl.when(sec < nsec - 1)
         def _():
             pass_copy(k, m).wait_recv()
+
+        for g in range(3):
+            store(g, k, m).wait()
+
+    for copy in rows_out:
+        copy.wait()
+
+    @pl.when(sec == nsec - 1)
+    def _():
+        clear().wait()
+
+
+def finish(pieces, *refs):
+    count = len(refs) // 2
+    sem = refs[-1]
+    copies = []
+    for g in range(count):
+        src, dst = refs[g], refs[count + g]
+        parts = pieces if src.shape[0] % pieces == 0 else 1
+        size = src.shape[0] // parts
+        for p in range(parts):
+            at = pl.ds(p * size, size)
+            copies.append(pltpu.make_async_copy(src.at[at], dst.at[at], sem.at[g, p]))
+    for copy in copies:
+        copy.start()
+    for copy in copies:
+        copy.wait()
 
 
 def shards(n, nsec, gate_q, gate_k, value_in, filter_raw, decay_rate, skip_gain, grad_out):
@@ -335,15 +431,23 @@
     fwd, inv = jnp.asarray(fwd, BF16), jnp.asarray(inv, BF16)
     block = jax.ShapeDtypeStruct((rows, channels), BF16)
     row = jax.ShapeDtypeStruct((1, channels), F32)
-    vmem = pl.BlockSpec(memory_space=pltpu.VMEM)
     message = (steps, n, rows, 3 * chunk)
     dma = pltpu.SemaphoreType.DMA
+    anywhere = pl.BlockSpec(memory_space=pl.ANY)
+    shapes = (block, block, block, block, row, row)
     outs = pl.pallas_call(
         functools.partial(kernel, n, nsec, chunk, steps),
-        out_shape=(block, block, block, block, row, row),
-        in_specs=[vmem] * 9,
-        out_specs=(vmem,) * 6,
+        out_shape=shapes,
+        in_specs=[anywhere] * 9,
+        out_specs=(anywhere,) * 6,
         scratch_shapes=[
+            *([pltpu.VMEM((rows, channels), BF16)] * 5),
+            *([pltpu.VMEM((1, channels), F32)] * 2),
+            *([pltpu.VMEM(fwd.shape, BF16)] * 2),
+            pltpu.VMEM((3, steps, n, rows, chunk), BF16),
+            pltpu.VMEM((rows, channels), BF16),
+            *([pltpu.VMEM((1, channels), F32)] * 2),
+            dma((5, 2, n)), dma((4,)), dma((3, steps, n)), dma((3,)),
             pltpu.VMEM(message, BF16),
             pltpu.VMEM(message, BF16),
             pltpu.VMEM(message, BF16),
@@ -357,14 +461,22 @@
             dma((steps, n)), dma((steps, n)), dma((n,)), dma((n,)),
         ],
         compiler_params=pltpu.CompilerParams(
-            collective_id=0, has_side_effects=True, vmem_limit_bytes=50 * 1024 * 1024
+            collective_id=0, has_side_effects=True, vmem_limit_bytes=58 * 1024 * 1024
         ),
         name="hyena_backward",
     )(
         gate_q[0], gate_k[0], value_in[0], filter_raw[0], grad_out[0],
         decay_rate, skip_gain, fwd, inv,
     )
-    oq, ok, op, of, orate, oskip = outs
+    pieces = 4
+    oq, ok, op, of, orate, oskip = pl.pallas_call(
+        functools.partial(finish, pieces),
+        out_shape=shapes,
+        in_specs=[anywhere] * 6,
+        out_specs=(anywhere,) * 6,
+        scratch_shapes=[dma((6, pieces))],
+        name="hand_over",
+    )(*outs)
     return oq[None], ok[None], op[None], of[None], orate, oskip
 
 

time: 94 us -> 210 us (2.23)
  Pallas kernels: 83 us -> 210 us
  local copies, waits for them, and re-layouts: 9.87 us -> 0 us
    pallas_call x0 -> x1, Pallas kernels: none -> 129 us  [shards(): pl.pallas_call(functools.partial(finish, pieces), out_shape=shapes, in_sp...]
    unnamed x18 -> x0, local copies, waits for them, and re-layouts: 9.87 us -> none
    pallas_call x1, Pallas kernels: 83 us -> 80.2 us  [shards(): pl.pallas_call(functools.partial(kernel, n, nsec, chunk, steps), out_shap...]
where the time goes in v2:
time: 210 us
  Pallas kernels  210 us (100%)
    pallas_call x1, Pallas kernels, shards(): pl.pallas_call(functools.partial(finish, pieces), out_shape=shapes, in_sp...  129 us
    pallas_call x1, Pallas kernels, shards(): pl.pallas_call(functools.partial(kernel, n, nsec, chunk, steps), out_shap...  80.2 us

profile of v2, /device:TPU:1, one launch (start us, length us, event | category | flops | bytes accessed | tf_op | source)
XLA Modules:
  0.0 210.3 jit_solution(13588082705645824749)
XLA Ops:
  0.6 80.2 %hyena_backward.1 = (bf16[128,4096]{1,0:T(8,128)(2,1)}, bf16[128,4096]{1,0:T(8,128)(2,1)}, bf16[128,4096]{1,0:T(8,128)(2,1)}, bf16[128,4096]{1,0:T(8,128)(2,1)}, f32[1,4096]{1,0:T(1,128)}, /*index=5*/f32[1,4096]{1,0:T(1,128)}) custom-call(bf16[128,4096]{1,0:T(8,128)(2,1)} %bitcast.9, bf16[128,4096]{1,0:T(8,128)(2,1)} %bitcast.10, ...), custom_call_target="tpu_custom_call" | custom-call | tf_op jit(solution)/shard_map/hyena_backward/pallas_call | solution.py:438
  80.9 129.4 %hand_over.1 = (bf16[128,4096]{1,0:T(8,128)(2,1)}, bf16[128,4096]{1,0:T(8,128)(2,1)}, bf16[128,4096]{1,0:T(8,128)(2,1)}, bf16[128,4096]{1,0:T(8,128)(2,1)}, f32[1,4096]{1,0:T(1,128)}, /*index=5*/f32[1,4096]{1,0:T(1,128)}) custom-call(bf16[128,4096]{1,0:T(8,128)(2,1)} %get-tuple-element.18.refs_0_, bf16[128,4096]{1,0:T(8,128)(2,1)} %get-tuple-element.19.refs_1_, ...), custom_call_target="tpu_custom_call" | custom-call | tf_op jit(solution)/shard_map/hand_over/pallas_call | solution.py:472

commit v3 on v2

--- a/solution.py
+++ b/solution.py
@@ -406,20 +406,26 @@
 
 
 def finish(pieces, *refs):
-    count = len(refs) // 2
-    sem = refs[-1]
+    count = (len(refs) - 2) // 3
+    load_sem, store_sem = refs[-2:]
     copies = []
     for g in range(count):
-        src, dst = refs[g], refs[count + g]
+        src, dst, held = refs[g], refs[count + g], refs[2 * count + g]
         parts = pieces if src.shape[0] % pieces == 0 else 1
         size = src.shape[0] // parts
         for p in range(parts):
             at = pl.ds(p * size, size)
-            copies.append(pltpu.make_async_copy(src.at[at], dst.at[at], sem.at[g, p]))
-    for copy in copies:
-        copy.start()
-    for copy in copies:
-        copy.wait()
+            copies.append((
+                pltpu.make_async_copy(src.at[at], held.at[at], load_sem.at[g, p]),
+                pltpu.make_async_copy(held.at[at], dst.at[at], store_sem.at[g, p]),
+            ))
+    for load, _ in copies:
+        load.start()
+    for load, store in copies:
+        load.wait()
+        store.start()
+    for _, store in copies:
+        store.wait()
 
 
 def shards(n, nsec, gate_q, gate_k, value_in, filter_raw, decay_rate, skip_gain, grad_out):
@@ -474,7 +480,10 @@
         out_shape=shapes,
         in_specs=[anywhere] * 6,
         out_specs=(anywhere,) * 6,
-        scratch_shapes=[dma((6, pieces))],
+        scratch_shapes=[
+            *(pltpu.VMEM(shape.shape, shape.dtype) for shape in shapes),
+            dma((6, pieces)), dma((6, pieces)),
+        ],
         name="hand_over",
     )(*outs)
     return oq[None], ok[None], op[None], of[None], orate, oskip

time: 210 us -> 85 us (0.40)
  Pallas kernels: 210 us -> 84.2 us
    pallas_call x1, Pallas kernels: 129 us -> 4 us  [shards(): pl.pallas_call(functools.partial(finish, pieces), out_shape=shapes, in_sp...]
where the time goes in v3:
time: 85 us; the launch traced here: 84.9 us
  Pallas kernels  84.2 us (99%)
    pallas_call x1, Pallas kernels, shards(): pl.pallas_call(functools.partial(kernel, n, nsec, chunk, steps), out_shap...  80.2 us
    pallas_call x1, Pallas kernels, shards(): pl.pallas_call(functools.partial(finish, pieces), out_shape=shapes, in_sp...  4 us

profile of v3, /device:TPU:1, one launch (start us, length us, event | category | flops | bytes accessed | tf_op | source)
XLA Modules:
  0.0 84.9 jit_solution(15124115628539270944)
XLA Ops:
  0.6 80.2 %hyena_backward.1 = (bf16[128,4096]{1,0:T(8,128)(2,1)}, bf16[128,4096]{1,0:T(8,128)(2,1)}, bf16[128,4096]{1,0:T(8,128)(2,1)}, bf16[128,4096]{1,0:T(8,128)(2,1)}, f32[1,4096]{1,0:T(1,128)}, /*index=5*/f32[1,4096]{1,0:T(1,128)}) custom-call(bf16[128,4096]{1,0:T(8,128)(2,1)} %bitcast.9, bf16[128,4096]{1,0:T(8,128)(2,1)} %bitcast.10, ...), custom_call_target="tpu_custom_call" | custom-call | tf_op jit(solution)/shard_map/hyena_backward/pallas_call | solution.py:444
  80.9 4.0 %hand_over.1 = (bf16[128,4096]{1,0:T(8,128)(2,1)}, bf16[128,4096]{1,0:T(8,128)(2,1)}, bf16[128,4096]{1,0:T(8,128)(2,1)}, bf16[128,4096]{1,0:T(8,128)(2,1)}, f32[1,4096]{1,0:T(1,128)}, /*index=5*/f32[1,4096]{1,0:T(1,128)}) custom-call(bf16[128,4096]{1,0:T(8,128)(2,1)} %get-tuple-element.18.refs_0_, bf16[128,4096]{1,0:T(8,128)(2,1)} %get-tuple-element.19.refs_1_, ...), custom_call_target="tpu_custom_call" | custom-call | tf_op jit(solution)/shard_map/hand_over/pallas_call | solution.py:478

commit v4 on v3

--- a/solution.py
+++ b/solution.py
@@ -126,9 +126,19 @@
         pl.semaphore_signal(
             barrier, inc=1, device_id={"ctx": lax.rem(me + o, n)}, device_id_type=MESH
         )
-    for other in (before, after):
-        pl.semaphore_signal(barrier, inc=1, device_id={"section": other}, device_id_type=MESH)
-    pl.semaphore_wait(barrier, n + 1)
+
+    @pl.when(sec < nsec - 1)
+    def _():
+        pl.semaphore_signal(barrier, inc=1, device_id={"section": after}, device_id_type=MESH)
+
+    @pl.when(sec > 0)
+    def _():
+        pl.semaphore_wait(barrier, n)
+
+    @pl.when(sec == 0)
+    def _():
+        pl.semaphore_wait(barrier, n - 1)
+
     load_whole(0).wait()
 
     def here(row0, count):

time: 85 us -> 85 us (level)
  no operation moved by 1% of the time
where the time goes in v4:
time: 85 us; the launch traced here: 84.9 us
  Pallas kernels  84.2 us (99%)
    pallas_call x1, Pallas kernels, shards(): pl.pallas_call(functools.partial(kernel, n, nsec, chunk, steps), out_shap...  80.2 us
    pallas_call x1, Pallas kernels, shards(): pl.pallas_call(functools.partial(finish, pieces), out_shape=shapes, in_sp...  4 us

profile of v4, /device:TPU:1, one launch (start us, length us, event | category | flops | bytes accessed | tf_op | source)
XLA Modules:
  0.0 84.9 jit_solution(15437428996994303405)
XLA Ops:
  0.6 80.2 %hyena_backward.1 = (bf16[128,4096]{1,0:T(8,128)(2,1)}, bf16[128,4096]{1,0:T(8,128)(2,1)}, bf16[128,4096]{1,0:T(8,128)(2,1)}, bf16[128,4096]{1,0:T(8,128)(2,1)}, f32[1,4096]{1,0:T(1,128)}, /*index=5*/f32[1,4096]{1,0:T(1,128)}) custom-call(bf16[128,4096]{1,0:T(8,128)(2,1)} %bitcast.9, bf16[128,4096]{1,0:T(8,128)(2,1)} %bitcast.10, ...), custom_call_target="tpu_custom_call" | custom-call | tf_op jit(solution)/shard_map/hyena_backward/pallas_call | solution.py:454
  80.9 4.0 %hand_over.1 = (bf16[128,4096]{1,0:T(8,128)(2,1)}, bf16[128,4096]{1,0:T(8,128)(2,1)}, bf16[128,4096]{1,0:T(8,128)(2,1)}, bf16[128,4096]{1,0:T(8,128)(2,1)}, f32[1,4096]{1,0:T(1,128)}, /*index=5*/f32[1,4096]{1,0:T(1,128)}) custom-call(bf16[128,4096]{1,0:T(8,128)(2,1)} %get-tuple-element.18.refs_0_, bf16[128,4096]{1,0:T(8,128)(2,1)} %get-tuple-element.19.refs_1_, ...), custom_call_target="tpu_custom_call" | custom-call | tf_op jit(solution)/shard_map/hand_over/pallas_call | solution.py:488
